TPU v7x, 256 devices: a whole 4x4x8 slice. The times are simulated.
256 devices in a mesh: chan: 8 (over x, core), filt: 32 (over y, z).
Axes of the slice: x: 4, y: 4, z: 8, core: 2. Of those that a mesh axis runs over, the one named last changes fastest.
Arguments:
- inputs: bfloat16 [1, 64, 128, 1024], P(None, 'filt', None, 'chan'), may hold values from -6 to 6
- weights: bfloat16 [3, 3, 1024, 1024], P(None, None, 'filt', 'chan'), may hold values from -0.0625 to 0.0625
- cotangent: bfloat16 [1, 64, 1024, 128], P(None, 'chan', 'filt'), may hold values from -6 to 6
Outputs:
- outputs: bfloat16 [1, 64, 1024, 128], P(None, 'chan', 'filt')
- input_grad: bfloat16 [1, 64, 128, 1024], P(None, 'filt', None, 'chan')
- weight_grad: float32 [3, 3, 1024, 1024], P(None, None, 'filt', 'chan')
All inputs are finite; a program needn't handle non-finite values.
Results may differ from a plain program's by a relative error of at most 0.001.
Values may be sent and summed in bfloat16 or wider, within the bound.
A program may use at most 128 MiB of HBM per device.

v0:
```python
import math
import jax
import jax.numpy as jnp
from jax import lax
from jax.sharding import PartitionSpec as P


def backward_taps(padded, kernel, row_count, col_count):
    summed = None
    for tap_row in range(3):
        for tap_col in range(3):
            source = padded[
                :, 2 - tap_row : 2 - tap_row + row_count, :, 2 - tap_col : 2 - tap_col + col_count
            ]
            product = jnp.einsum(
                "bhfw,fc->bhwc",
                source,
                kernel[tap_row, tap_col],
                preferred_element_type=jnp.float32,
            )
            summed = product if summed is None else summed + product
    return summed


def body(inputs, weights, cotangent):
    gathered = lax.all_gather(inputs, "filt", axis=1, tiled=True)
    cot_all = lax.all_gather(cotangent, "chan", axis=1, tiled=True)
    row_count = gathered.shape[1]
    col_count = gathered.shape[2]
    padded_in = jnp.pad(gathered, ((0, 0), (1, 1), (1, 1), (0, 0)))
    norm_factor = 1.0 / math.sqrt(gathered.shape[0] * row_count * col_count)
    summed_out = None
    grad_taps = []
    for tap_row in range(3):
        for tap_col in range(3):
            source = padded_in[:, tap_row : tap_row + row_count, tap_col : tap_col + col_count, :]
            product = jnp.einsum(
                "bhwc,fc->bhwf",
                source,
                weights[tap_row, tap_col],
                preferred_element_type=jnp.float32,
            )
            summed_out = product if summed_out is None else summed_out + product
            grad_taps.append(
                jnp.einsum("bhwc,bhfw->fc", source, cot_all, preferred_element_type=jnp.float32)
                * norm_factor
            )
    partial_out = jnp.transpose(summed_out, (0, 1, 3, 2))
    outputs = lax.psum_scatter(partial_out, "chan", scatter_dimension=1, tiled=True).astype(
        jnp.bfloat16
    )
    weight_grad = jnp.stack(grad_taps).reshape(3, 3, weights.shape[2], weights.shape[3])
    padded_cot = jnp.pad(cot_all, ((0, 0), (1, 1), (0, 0), (1, 1)))
    partial_grad = backward_taps(padded_cot, weights, row_count, col_count)
    input_grad = lax.psum_scatter(partial_grad, "filt", scatter_dimension=1, tiled=True).astype(
        jnp.bfloat16
    )
    return (outputs, input_grad, weight_grad)


def solution(mesh):
    return jax.shard_map(
        body,
        mesh=mesh,
        in_specs=(
            P(None, "filt", None, "chan"),
            P(None, None, "filt", "chan"),
            P(None, "chan", "filt", None),
        ),
        out_specs=(
            P(None, "chan", "filt", None),
            P(None, "filt", None, "chan"),
            P(None, None, "filt", "chan"),
        ),
        check_vma=False,
    )
```

profile of v0, /device:TPU:2, one launch (start us, length us, event | category | flops | bytes accessed | tf_op | source)
XLA Modules:
  0.0 368.4 jit_solution(7794976326158176993)
XLA Ops:
  7.2 0.7 all-gather.2.cloned.1.call-update
  7.9 13.4 %all_gather.7 = bf16[1,64,32,128]{3,2,0,1:T(8,128)(2,1)S(1)} all-gather(bf16[1,8,32,128]{3,2,0,1:T(8,128)(2,1)} %bitcast.402), channel_id=1, replica_groups=mesh['chan'=8,'filt'=32] {'chan'}, dimensions={1}, use_global_device_ids=true | all-gather | bytes 589824 | tf_op jit(solution)/shard_map/all_gather | solution.py:27
  21.3 3.8 %fusion.188 = f32[64,128,128]{2,1,0:T(8,128)} fusion(bf16[1,64,32,128]{3,2,1,0:T(8,128)(2,1)S(1)} %bitcast.394, bf16[3,3,32,128]{3,2,1,0:T(8,128)(2,1)} %param.4), kind=kOutput, calls=%fused_computation.107 | convolution fusion | flops 67108864 | bytes 4726784 | tf_op jit(solution)/shard_map/bhfw,fc->bhwc/dot_general | solution.py:15
  25.1 2.7 fusion.191
  27.8 3.0 fusion.194
  30.8 3.0 fusion.197
  33.9 3.0 fusion.200
  36.9 54.9 %all-gather.2.cloned.1.call-done = bf16[1,64,128,128]{3,2,0,1:T(8,128)(2,1)} async-done(((bf16[1,2,128,128]{3,2,0,1:T(8,128)(2,1)}), bf16[1,64,128,128]{3,2,0,1:T(8,128)(2,1)}) %all-gather.2.cloned.1.call-update) | async-done | bytes 2097168 | tf_op jit(solution)/shard_map/all_gather | solution.py:26
  91.8 2.5 fusion.26
  94.3 0.8 fusion.30
  95.1 0.8 fusion.10
  96.0 0.8 fusion.2
  96.8 0.8 fusion.55
  97.6 0.8 fusion.18
  98.4 0.8 fusion.61
  99.3 0.8 fusion.67
  100.1 1.8 fusion.76
  102.2 3.0 fusion.203
  105.2 2.7 fusion.206
  108.0 2.7 fusion.219
  110.7 0.7 copy-done.1
  111.4 10.6 %add_bitcast_fusion = f32[1,64,128,128]{3,2,1,0:T(8,128)} fusion(f32[64,128,128]{2,1,0:T(8,128)} %fusion.206, f32[64,128,128]{2,1,0:T(8,128)} %fusion.203, f32[64,128,128]{2,1,0:T(8,128)} %fusion.200, f32[64,128,128]{2,1,0:T(8,128)} %fusion.219, f32[64,128,128]{2,1,0:T(8,128)} %fusion.197, f32[64,128,128]{2,1,0:T(8,128)S(1)} %copy-done.3, ...), kind=kOutput, calls=%fused_computation | convolution fusion | flops 75497472 | bytes 38281216 | tf_op jit(solution)/shard_map/bhfw,fc->bhwc/dot_general | solution.py:15
  122.0 0.7 fusion.175
  123.2 0.8 fusion.157
  124.0 0.8 fusion.148
  125.2 0.8 fusion.139
  126.0 0.8 fusion.130
  127.3 0.8 fusion.112
  128.0 2.8 reduce-scatter.3.cloned.1.call-done
  130.9 1.5 convert_element_type.10
  132.4 227.9 %reduce-scatter.5.cloned.1.call-done = f32[1,2,128,128]{3,2,1,0:T(8,128)} async-done(((f32[1,64,128,128]{3,2,1,0:T(8,128)}), f32[1,2,128,128]{3,2,1,0:T(8,128)}) %reduce-scatter.5.cloned.1.call-update) | async-done | bytes 131088 | tf_op jit(solution)/shard_map/reduce_scatter | solution.py:55
  360.3 1.5 convert_element_type.11
  (19 shorter events, 1.8 us)
Async XLA Ops:
  7.2 84.6 %all-gather.2.cloned.1.call-start = ((), (), s32[]{:S(2)}) async-start(), calls=%async_computation.2 | async-start | bytes 2162688 | tf_op jit(solution)/shard_map/all_gather | solution.py:26
  7.9 123.0 %reduce-scatter.3.cloned.1.call-start = ((), (), s32[]{:S(2)}) async-start(), calls=%async_computation.3 | async-start | bytes 1179648 | tf_op jit(solution)/shard_map/reduce_scatter | solution.py:49
  21.3 3.8 %copy-start.4 = (bf16[3,3,32,128]{3,2,1,0:T(8,128)(2,1)S(1)}, bf16[3,3,32,128]{3,2,1,0:T(8,128)(2,1)}, u32[]{:S(2)}) copy-start(bf16[3,3,32,128]{3,2,1,0:T(8,128)(2,1)} %param.4) | copy-start | bytes 221188
  91.8 2.6 copy-start
  102.0 258.3 %reduce-scatter.5.cloned.1.call-start = ((), (), s32[]{:S(2)}) async-start(), calls=%async_computation.4 | async-start | bytes 4325376 | tf_op jit(solution)/shard_map/reduce_scatter | solution.py:55
  102.2 8.5 %copy-start.3 = (f32[64,128,128]{2,1,0:T(8,128)S(1)}, f32[64,128,128]{2,1,0:T(8,128)}, u32[]{:S(2)}) copy-start(f32[64,128,128]{2,1,0:T(8,128)} %fusion.194) | copy-start | bytes 12582916
  105.2 5.5 %copy-start.2 = (f32[64,128,128]{2,1,0:T(8,128)S(1)}, f32[64,128,128]{2,1,0:T(8,128)}, u32[]{:S(2)}) copy-start(f32[64,128,128]{2,1,0:T(8,128)} %fusion.191) | copy-start | bytes 12582916
  108.0 3.4 copy-start.1
  128.0 233.9 %copy-start.5 = (f32[9,32,128]{2,1,0:T(8,128)}, f32[9,32,128]{2,1,0:T(8,128)S(1)}, u32[]{:S(2)}) copy-start(f32[9,32,128]{2,1,0:T(8,128)S(1)} %fusion.112) | copy-start | bytes 442372
Sparse Core Ops, SparseCore 0:
  10.6 81.1 all-gather.1
  102.1 28.7 reduce-scatter.2
  134.8 225.5 reduce-scatter.4
where the time goes:
time: 369 us; the launch traced here: 368 us
  waiting for transfers between devices  286 us (78%)
  matrix products  50.8 us (14%)
  between operations  13.8 us (4%)
  blocking collectives  13.4 us (4%)
    reduce_scatter x1, waiting for transfers between devices, body(): lax.psum_scatter(partial_grad, 'filt', scatter_dimension=1, tiled=True)  228 us
    all_gather x1, waiting for transfers between devices, body(): gathered = lax.all_gather(inputs, 'filt', axis=1, tiled=True)  54.9 us
    dot_general x9, matrix products, backward_taps(): jnp.einsum('bhfw,fc->bhwc', source, kernel[tap_row, tap_col], preferred_e...  34.6 us
    all_gather x1, blocking collectives, body(): cot_all = lax.all_gather(cotangent, 'chan', axis=1, tiled=True)  13.4 us
    dot_general x9, matrix products, body(): jnp.einsum('bhwc,fc->bhwf', source, weights[tap_row, tap_col], preferred_...  10.2 us
  transfers between devices with their start and end apart: 3, of which 3 were waited for; matrix products, arithmetic and copies ran while one was open for 11% of the time, Pallas kernels for 0%

commit v1 on v0

--- a/solution.py
+++ b/solution.py
@@ -23,7 +23,8 @@
 
 
 def body(inputs, weights, cotangent):
-    gathered = lax.all_gather(inputs, "filt", axis=1, tiled=True)
+    sent = jnp.stack([inputs] * lax.axis_size("filt"))
+    gathered = jnp.concatenate(lax.all_to_all(sent, "filt", 0, 0), axis=1)
     cot_all = lax.all_gather(cotangent, "chan", axis=1, tiled=True)
     row_count = gathered.shape[1]
     col_count = gathered.shape[2]

time: 369 us -> 348 us (0.943)
  waiting for transfers between devices: 286 us -> 254 us
  starting transfers between devices: 0.3 us -> 11.9 us
    all_gather x1 -> x0, waiting for transfers between devices: 54.9 us -> none  [body(): gathered = lax.all_gather(inputs, 'filt', axis=1, tiled=True)]
    all_to_all x0 -> x1, waiting for transfers between devices: none -> 22.1 us  [body(): gathered = jnp.concatenate(lax.all_to_all(sent, 'filt', 0, 0), axis=1)]
    all_to_all x0 -> x1, starting transfers between devices: none -> 11.6 us  [body(): gathered = jnp.concatenate(lax.all_to_all(sent, 'filt', 0, 0), axis=1)]
  transfers between devices with their start and end apart: 3 -> 3, of which waited for: 3 -> 3; matrix products, arithmetic and copies ran while one was open for 11% -> 12% of each run, Pallas kernels for 0% -> 0%
where the time goes in v1:
time: 348 us; the launch traced here: 347 us
  waiting for transfers between devices  254 us (73%)
  matrix products  48.3 us (14%)
  between operations  14.1 us (4%)
  blocking collectives  13.2 us (4%)
  starting transfers between devices  11.9 us (3%)
    reduce_scatter x1, waiting for transfers between devices, body(): lax.psum_scatter(partial_grad, 'filt', scatter_dimension=1, tiled=True)  228 us
    dot_general x9, matrix products, backward_taps(): jnp.einsum('bhfw,fc->bhwc', source, kernel[tap_row, tap_col], preferred_e...  33.9 us
    all_to_all x1, waiting for transfers between devices, body(): gathered = jnp.concatenate(lax.all_to_all(sent, 'filt', 0, 0), axis=1)  22.1 us
    all_gather x1, blocking collectives, body(): cot_all = lax.all_gather(cotangent, 'chan', axis=1, tiled=True)  13.2 us
    all_to_all x1, starting transfers between devices, body(): gathered = jnp.concatenate(lax.all_to_all(sent, 'filt', 0, 0), axis=1)  11.6 us
    dot_general x9, matrix products, body(): jnp.einsum('bhwc,fc->bhwf', source, weights[tap_row, tap_col], preferred_...  8.45 us
  transfers between devices with their start and end apart: 3, of which 3 were waited for; matrix products, arithmetic and copies ran while one was open for 12% of the time, Pallas kernels for 0%

profile of v1, /device:TPU:2, one launch (start us, length us, event | category | flops | bytes accessed | tf_op | source)
XLA Modules:
  0.0 347.5 jit_solution(17322843580735847765)
XLA Ops:
  7.2 2.7 stack.22
  9.9 11.6 %all-to-all-start = ((bf16[32,1,2,128,128]{4,3,2,1,0:T(8,128)(2,1)}), bf16[32,1,2,128,128]{4,3,2,1,0:T(8,128)(2,1)S(1)}, u32[]{:S(2)}, u32[]{:S(2)}) async-start(bf16[32,1,2,128,128]{4,3,2,1,0:T(8,128)(2,1)} %stack.22), calls=%async_computation | async-start | bytes 4194304 | tf_op jit(solution)/shard_map/all_to_all | solution.py:27
  21.5 13.2 %all_gather.3 = bf16[1,64,32,128]{3,2,0,1:T(8,128)(2,1)S(1)} all-gather(bf16[1,8,32,128]{3,2,0,1:T(8,128)(2,1)S(1)} %bitcast.395), channel_id=1, replica_groups=mesh['chan'=8,'filt'=32] {'chan'}, dimensions={1}, use_global_device_ids=true | all-gather | bytes 589824 | tf_op jit(solution)/shard_map/all_gather | solution.py:28
  34.7 3.0 fusion.175
  37.7 2.7 fusion.178
  40.4 3.0 fusion.181
  43.4 3.0 fusion.184
  46.5 3.0 fusion.187
  49.5 22.1 %all-to-all-done = bf16[32,1,2,128,128]{4,3,2,1,0:T(8,128)(2,1)S(1)} async-done(((bf16[32,1,2,128,128]{4,3,2,1,0:T(8,128)(2,1)}), bf16[32,1,2,128,128]{4,3,2,1,0:T(8,128)(2,1)S(1)}, u32[]{:S(2)}, u32[]{:S(2)}) %all-to-all-start) | async-done | bytes 2097184 | tf_op jit(solution)/shard_map/all_to_all | solution.py:27
  71.5 0.8 fusion.22
  72.3 0.8 fusion.26
  73.2 0.8 fusion.10
  74.0 0.8 fusion.2
  74.8 0.8 fusion.217
  75.6 0.8 fusion.51
  76.5 0.8 fusion.57
  77.3 0.8 fusion.63
  78.2 1.8 fusion.72
  80.3 3.0 fusion.190
  83.2 2.7 fusion.193
  86.0 2.7 fusion.206
  89.4 10.6 %add_bitcast_fusion = f32[1,64,128,128]{3,2,1,0:T(8,128)} fusion(f32[64,128,128]{2,1,0:T(8,128)} %fusion.193, f32[64,128,128]{2,1,0:T(8,128)} %fusion.190, f32[64,128,128]{2,1,0:T(8,128)} %fusion.187, f32[64,128,128]{2,1,0:T(8,128)} %fusion.206, f32[64,128,128]{2,1,0:T(8,128)} %fusion.184, f32[64,128,128]{2,1,0:T(8,128)S(1)} %copy-done.2, ...), kind=kOutput, calls=%fused_computation | convolution fusion | flops 75497472 | bytes 38281216 | tf_op jit(solution)/shard_map/bhfw,fc->bhwc/dot_general | solution.py:15
  100.0 0.7 fusion.171
  101.2 0.8 fusion.153
  102.0 0.8 fusion.144
  103.2 0.8 fusion.135
  104.0 0.8 fusion.126
  105.3 0.8 fusion.108
  106.0 3.4 reduce-scatter.3.cloned.1.call-done
  109.5 1.5 convert_element_type.10
  111.0 228.1 %reduce-scatter.5.cloned.1.call-done = f32[1,2,128,128]{3,2,1,0:T(8,128)} async-done(((f32[1,64,128,128]{3,2,1,0:T(8,128)}), f32[1,2,128,128]{3,2,1,0:T(8,128)}) %reduce-scatter.5.cloned.1.call-update) | async-done | bytes 131088 | tf_op jit(solution)/shard_map/reduce_scatter | solution.py:56
  339.1 1.5 convert_element_type.11
  (19 shorter events, 2.4 us)
Async XLA Ops:
  9.9 11.7 %copy-start.4 = (bf16[1,8,32,128]{3,2,1,0:T(8,128)(2,1)S(1)}, bf16[1,8,32,128]{3,2,1,0:T(8,128)(2,1)}, u32[]{:S(2)}) copy-start(bf16[1,8,32,128]{3,2,1,0:T(8,128)(2,1)} %param.5) | copy-start | bytes 196612
  9.9 24.9 %copy-start.3 = (bf16[3,3,32,128]{3,2,1,0:T(8,128)(2,1)S(1)}, bf16[3,3,32,128]{3,2,1,0:T(8,128)(2,1)}, u32[]{:S(2)}) copy-start(bf16[3,3,32,128]{3,2,1,0:T(8,128)(2,1)} %param.4) | copy-start | bytes 221188
  9.9 61.7 %all-to-all-start = ((bf16[32,1,2,128,128]{4,3,2,1,0:T(8,128)(2,1)}), bf16[32,1,2,128,128]{4,3,2,1,0:T(8,128)(2,1)S(1)}, u32[]{:S(2)}, u32[]{:S(2)}) async-start(bf16[32,1,2,128,128]{4,3,2,1,0:T(8,128)(2,1)} %stack.22), calls=%async_computation | async-start | bytes 4194304 | tf_op jit(solution)/shard_map/all_to_all | solution.py:27
  21.5 88.0 %reduce-scatter.3.cloned.1.call-start = ((), (), s32[]{:S(2)}) async-start(), calls=%async_computation.3 | async-start | bytes 1179648 | tf_op jit(solution)/shard_map/reduce_scatter | solution.py:50
  80.0 259.1 %reduce-scatter.5.cloned.1.call-start = ((), (), s32[]{:S(2)}) async-start(), calls=%async_computation.4 | async-start | bytes 4325376 | tf_op jit(solution)/shard_map/reduce_scatter | solution.py:56
  80.2 8.5 %copy-start.2 = (f32[64,128,128]{2,1,0:T(8,128)S(1)}, f32[64,128,128]{2,1,0:T(8,128)}, u32[]{:S(2)}) copy-start(f32[64,128,128]{2,1,0:T(8,128)} %fusion.181) | copy-start | bytes 12582916
  83.2 5.5 %copy-start.1 = (f32[64,128,128]{2,1,0:T(8,128)S(1)}, f32[64,128,128]{2,1,0:T(8,128)}, u32[]{:S(2)}) copy-start(f32[64,128,128]{2,1,0:T(8,128)} %fusion.178) | copy-start | bytes 12582916
  86.0 3.4 copy-start
  106.0 234.6 %copy-start.5 = (f32[9,32,128]{2,1,0:T(8,128)}, f32[9,32,128]{2,1,0:T(8,128)S(1)}, u32[]{:S(2)}) copy-start(f32[9,32,128]{2,1,0:T(8,128)S(1)} %fusion.108) | copy-start | bytes 442372
Sparse Core Ops, SparseCore 0:
  80.1 29.2 reduce-scatter.2
  113.4 225.6 reduce-scatter.4
